TPU v7x, 32 devices: a whole 2x2x4 slice. The times are simulated.
32 devices in a mesh: rows: 16 (over z, y, core), cols: 2 (over x).
Axes of the slice: x: 2, y: 2, z: 4, core: 2. Of those that a mesh axis runs over, the one named last changes fastest.
Arguments:
- matrix: float32 [8192, 8192], P('rows', 'cols'), may hold values from -6 to 6
- starts: int32 [4, 4], replicated, may hold values from 0 to 7936, as said below
- factors: float32 [4, 4, 256, 256], P(None, None, 'rows', 'cols'), as said below
Outputs:
- updated: float32 [8192, 8192], P('rows', 'cols')
Inputs may be any that keep to these rules, and one draw needn't show every extreme that they name: `starts`: every start is a multiple of 128; chain c's start lies in the c-th of 4 equal ranges of blocks and never decreases from advance to advance; a window may end on the first block of the next range; the windows of one advance are disjoint. `factors`: every factor is orthogonal.
All inputs are finite; a program needn't handle non-finite values.
Results may differ from a plain program's by a relative error of at most 0.0001.
Values sent between devices are 32-bit elements; how exact they have to be, the bound alone decides.
A program may use at most 128 MiB of HBM per device.

v0:
```python
import functools

import jax
import jax.numpy as jnp
from jax import lax
from jax.experimental import pallas as pl
from jax.experimental.pallas import tpu as pltpu
from jax.sharding import PartitionSpec as P

NB = 128
VMEM_LIMIT = 60 * 1024 * 1024


def split(value):
    high = value.astype(jnp.bfloat16)
    low = (value - high.astype(jnp.float32)).astype(jnp.bfloat16)
    return high, low


def product(left, right, dims):
    lh, ll = split(left)
    rh, rl = split(right)
    dot = functools.partial(
        lax.dot_general, dimension_numbers=(dims, ((), ())), preferred_element_type=jnp.float32
    )
    return dot(lh, rh) + (dot(lh, rl) + dot(ll, rh))


def pack_kernel(slots, tile_ref, out_ref):
    out_ref[0] = tile_ref[...]


def pack_columns(tile, slots, part, parts):
    rows = tile.shape[0] // parts
    count = slots.shape[0]
    return pl.pallas_call(
        pack_kernel,
        out_shape=jax.ShapeDtypeStruct((count, rows, NB), tile.dtype),
        grid_spec=pltpu.PrefetchScalarGridSpec(
            num_scalar_prefetch=1,
            grid=(count,),
            in_specs=[pl.BlockSpec((rows, NB), lambda w, slots: (part, slots[w]))],
            out_specs=pl.BlockSpec((1, rows, NB), lambda w, slots: (w, 0, 0)),
        ),
        cost_estimate=pl.CostEstimate(
            flops=0, transcendentals=0, bytes_accessed=8 * count * rows * NB
        ),
        name="pack_columns",
    )(slots, tile)


def column_kernel(slots, ghosts, heads, tile_ref, ghost_ref, factor_ref, out_ref, held):
    out_ref[...] = tile_ref[...]
    held[...] = ghost_ref[...]

    def step(w, carry):
        at = pl.multiple_of(slots[w] * NB, NB)
        ghost = ghosts[w]
        head = heads[w]
        own_rows = pl.multiple_of((1 - head) * NB, NB)
        other_rows = pl.multiple_of(head * NB, NB)
        window = jnp.concatenate([out_ref[:, pl.ds(at, NB)], held[ghost]], axis=1)
        factor = jnp.concatenate(
            [factor_ref[w, pl.ds(own_rows, NB), :], factor_ref[w, pl.ds(other_rows, NB), :]], axis=0
        )
        turned = product(window, factor, ((1,), (0,)))
        first, second = turned[:, :NB], turned[:, NB:]
        is_head = head == 1
        out_ref[:, pl.ds(at, NB)] = jnp.where(is_head, first, second)
        held[ghost] = jnp.where(is_head, second, first)
        return carry

    lax.fori_loop(0, factor_ref.shape[0], step, 0)


def turn_columns(tile, ghost, factors, slots, ghosts, heads, part):
    width = tile.shape[1]
    count, rows, _ = ghost.shape
    order = factors.shape[-1]
    return pl.pallas_call(
        column_kernel,
        out_shape=jax.ShapeDtypeStruct((rows, width), tile.dtype),
        grid_spec=pltpu.PrefetchScalarGridSpec(
            num_scalar_prefetch=3,
            grid=(1,),
            in_specs=[
                pl.BlockSpec((rows, width), lambda i, *_: (part, 0)),
                pl.BlockSpec((count, rows, NB), lambda i, *_: (0, 0, 0)),
                pl.BlockSpec((count, order, order), lambda i, *_: (0, 0, 0)),
            ],
            out_specs=pl.BlockSpec((rows, width), lambda i, *_: (0, 0)),
            scratch_shapes=[pltpu.VMEM((count, rows, NB), tile.dtype)],
        ),
        compiler_params=pltpu.CompilerParams(vmem_limit_bytes=VMEM_LIMIT),
        cost_estimate=pl.CostEstimate(
            flops=6 * count * rows * order * order,
            transcendentals=0,
            bytes_accessed=4 * (2 * rows * width + count * rows * NB + count * order * order),
        ),
        name="turn_columns",
    )(slots, ghosts, heads, tile, ghost, factors)


def exchange_columns(tile, blocks, parts):
    position = lax.axis_index("cols")
    heads = (blocks % 2 == position).astype(jnp.int32)
    own = blocks + 1 - heads
    other = blocks + heads
    slots = own // 2
    same = other[:, None] == other[None, :]
    ghosts = jnp.argmax(same, axis=1).astype(jnp.int32)
    packed, came = [], []
    for part in range(parts):
        packed.append(pack_columns(tile, slots, part, parts))
        came.append(lax.ppermute(packed[part], "cols", [(0, 1), (1, 0)]))
    return packed, came, (slots, ghosts, heads)


def from_behind(value, axis, steps):
    count = lax.axis_size(axis)
    pairs = [(source, (source + steps) % count) for source in range(count)]
    return lax.ppermute(value, axis, pairs)


def columns_of_many(tile, blocks, whole_factors, chains):
    position = lax.axis_index("cols")
    devices = lax.axis_size("cols")

    def owned(ids):
        parts, places = [], []
        for block in ids:
            start = block // devices * NB
            mine = block % devices == position
            part = lax.dynamic_slice_in_dim(tile, start, NB, 1)
            parts.append(jnp.where(mine, part, jnp.zeros_like(part)))
            places.append((start, mine))
        return jnp.stack(parts), places

    for first in range(0, blocks.shape[0], chains):
        ids = [blocks[first + c] for c in range(chains)]
        left, left_places = owned(ids)
        right, right_places = owned([block + 1 for block in ids])
        window = jnp.concatenate(
            [left + from_behind(left, "cols", 1), right + from_behind(right, "cols", -1)], axis=2
        )
        turned = jnp.einsum(
            "crj,cji->cri",
            window,
            whole_factors[first : first + chains],
            precision=lax.Precision.HIGHEST,
            preferred_element_type=jnp.float32,
        )
        for c in range(chains):
            for (start, mine), new in (
                (left_places[c], turned[c, :, :NB]),
                (right_places[c], turned[c, :, NB:]),
            ):
                now = lax.dynamic_slice_in_dim(tile, start, NB, 1)
                tile = lax.dynamic_update_slice_in_dim(tile, jnp.where(mine, new, now), start, 1)
    return tile


def plan_kernel(devices, slots, count, blocks, me_ref, plan):
    me = me_ref[0]

    def clear(t, carry):
        for row in range(slots + 1):
            plan[row, t] = -1
        for row in range(slots + 1, slots + 4):
            plan[row, t] = 0
        return carry

    lax.fori_loop(0, count, clear, 0)
    block = [blocks[w] for w in range(count)]
    owner = [lax.rem(b, devices) for b in block]
    when = []
    for w in range(count):
        odd = lax.rem(owner[w], 2)
        step = odd
        for v in range(w):
            clash = (
                (block[w] == block[v])
                | (block[w] == block[v] + 1)
                | (block[w] + 1 == block[v])
                | ((owner[w] == owner[v]) & (odd == 1))
            )
            step = jnp.maximum(step, jnp.where(clash, when[v] + 1, 0))
        when.append(step)
        kind = jnp.where(odd == 0, 1, jnp.where(lax.rem(owner[w], 4) == 1, 2, 4))
        plan[slots + 2, step] = plan[slots + 2, step] | kind
        plan[slots + 3, 0] = jnp.maximum(plan[slots + 3, 0], step + 1)
        is_head = owner[w] == me

        @pl.when(is_head | (lax.rem(owner[w] + 1, devices) == me))
        def _():
            slot = jnp.where(is_head, block[w], block[w] + 1) // devices
            row = jnp.where(odd == 1, slots, slot)
            plan[row, step] = 2 * w + is_head.astype(jnp.int32)
            plan[slots + 1, step] = jnp.where(odd == 1, slot, plan[slots + 1, step])


def make_plan(blocks, me, devices, slots):
    count = blocks.shape[0]
    smem = pl.BlockSpec(memory_space=pltpu.SMEM)
    return pl.pallas_call(
        functools.partial(plan_kernel, devices, slots, count),
        out_shape=jax.ShapeDtypeStruct((slots + 4, count), jnp.int32),
        in_specs=[smem, smem],
        out_specs=smem,
        name="plan_steps",
    )(blocks, me.reshape(1))


def turn_block(code, job, mine, ghost, factor, pieces, chunk):
    head = lax.rem(code, 2)
    near = pl.multiple_of((1 - head) * NB, NB)
    far = pl.multiple_of(head * NB, NB)
    turn = jnp.concatenate(
        [
            factor[job, pl.ds(near, NB), pl.ds(near, NB)],
            factor[job, pl.ds(far, NB), pl.ds(near, NB)],
        ],
        axis=0,
    ).T

    def piece(j, carry):
        at = pl.ds(pl.multiple_of(j * chunk, NB), chunk)
        window = jnp.concatenate([mine[job, :, at], ghost[job, :, at]], axis=0)
        mine[job, :, at] = product(turn, window, ((1,), (0,)))
        return carry

    lax.fori_loop(0, pieces, piece, 0)


def row_kernel(
    slots, pieces, plan, t_ref, tile, even, odd, factors, out,
    mine, ghost, factor, mine_sem, ghost_sem, factor_sem, out_sem,
):
    t = t_ref[0]
    width = mine.shape[2]
    chunk = width // pieces
    jobs = slots + 1

    def place(job):
        slot = job if job < slots else plan[slots + 1, t]
        return pl.ds(pl.multiple_of(slot * NB, NB), NB)

    def loads(job):
        code = jnp.maximum(plan[job, t], 0)
        source = even.at[pl.ds(job * NB, NB), :] if job < slots else odd
        return (
            pltpu.make_async_copy(tile.at[place(job), :], mine.at[job], mine_sem.at[job]),
            pltpu.make_async_copy(source, ghost.at[job], ghost_sem.at[job]),
            pltpu.make_async_copy(factors.at[code // 2], factor.at[job], factor_sem.at[job]),
        )

    def store(job):
        return pltpu.make_async_copy(mine.at[job], out.at[place(job), :], out_sem.at[job])

    for job in range(jobs):

        @pl.when(plan[job, t] >= 0)
        def _():
            for copy in loads(job):
                copy.start()

    for job in range(jobs):

        @pl.when(plan[job, t] >= 0)
        def _():
            for copy in loads(job):
                copy.wait()
            turn_block(plan[job, t], job, mine, ghost, factor, pieces, chunk)
            store(job).start()

    for job in range(jobs):

        @pl.when(plan[job, t] >= 0)
        def _():
            store(job).wait()


def turn_rows(plan, t, tile, even, odd, factors):
    width = tile.shape[1]
    slots = tile.shape[0] // NB
    jobs = slots + 1
    order = factors.shape[-1]
    pieces = 4 if width % (4 * NB) == 0 else 1
    smem = pl.BlockSpec(memory_space=pltpu.SMEM)
    any_space = pl.BlockSpec(memory_space=pl.ANY)
    return pl.pallas_call(
        functools.partial(row_kernel, slots, pieces),
        out_shape=jax.ShapeDtypeStruct(tile.shape, tile.dtype),
        in_specs=[smem, smem] + [any_space] * 4,
        out_specs=any_space,
        scratch_shapes=[
            pltpu.VMEM((jobs, NB, width), tile.dtype),
            pltpu.VMEM((jobs, NB, width), tile.dtype),
            pltpu.VMEM((jobs, order, order), tile.dtype),
        ]
        + [pltpu.SemaphoreType.DMA((jobs,))] * 4,
        input_output_aliases={2: 0},
        compiler_params=pltpu.CompilerParams(vmem_limit_bytes=VMEM_LIMIT),
        name="turn_rows",
    )(plan, t.reshape(1), tile, even, odd, factors)


def even_kernel(base, pieces, plan, part, even, factors, *rest):
    out, mine, ghost, factor, mine_sem, ghost_sem, factor_sem, out_sem = rest[-8:]
    jobs, _, width = mine.shape
    chunk = width // pieces

    def load(job):
        return pltpu.make_async_copy(
            part.at[pl.ds(job * NB, NB), :], mine.at[job], mine_sem.at[job]
        )

    def others(job):
        code = jnp.maximum(plan[base + job, 0], 0)
        return (
            pltpu.make_async_copy(
                even.at[pl.ds(job * NB, NB), :], ghost.at[job], ghost_sem.at[job]
            ),
            pltpu.make_async_copy(factors.at[code // 2], factor.at[job], factor_sem.at[job]),
        )

    def store(job):
        return pltpu.make_async_copy(
            mine.at[job], out.at[pl.ds((base + job) * NB, NB), :], out_sem.at[job]
        )

    for job in range(jobs):
        load(job).start()

        @pl.when(plan[base + job, 0] >= 0)
        def _():
            for copy in others(job):
                copy.start()

    for job in range(jobs):
        load(job).wait()

        @pl.when(plan[base + job, 0] >= 0)
        def _():
            for copy in others(job):
                copy.wait()
            turn_block(plan[base + job, 0], job, mine, ghost, factor, pieces, chunk)

        store(job).start()
    for job in range(jobs):
        store(job).wait()


def turn_even(plan, part, even, factors, base, slots, tile=None):
    rows, width = part.shape
    jobs = rows // NB
    order = factors.shape[-1]
    pieces = 4 if width % (4 * NB) == 0 else 1
    any_space = pl.BlockSpec(memory_space=pl.ANY)
    extra = () if tile is None else (tile,)
    return pl.pallas_call(
        functools.partial(even_kernel, base, pieces),
        out_shape=jax.ShapeDtypeStruct((slots * NB, width), part.dtype),
        in_specs=[pl.BlockSpec(memory_space=pltpu.SMEM)] + [any_space] * (3 + len(extra)),
        out_specs=any_space,
        scratch_shapes=[
            pltpu.VMEM((jobs, NB, width), part.dtype),
            pltpu.VMEM((jobs, NB, width), part.dtype),
            pltpu.VMEM((jobs, order, order), part.dtype),
        ]
        + [pltpu.SemaphoreType.DMA((jobs,))] * 4,
        input_output_aliases={} if tile is None else {4: 0},
        compiler_params=pltpu.CompilerParams(vmem_limit_bytes=VMEM_LIMIT),
        cost_estimate=pl.CostEstimate(
            flops=6 * rows * 2 * NB * width, transcendentals=0, bytes_accessed=12 * rows * width
        ),
        name="turn_even",
    )(plan, part, even, factors, *extra)


def unset(shape, dtype):
    return pl.pallas_call(
        lambda out: None,
        out_shape=jax.ShapeDtypeStruct(shape, dtype),
        out_specs=pl.BlockSpec(memory_space=pl.ANY),
        name="unset",
    )()


def turn_all_rows(plan, column_parts, slots, whole_factors):
    devices = lax.axis_size("rows")

    def pairs(lows):
        ways = []
        for low in lows:
            high = (low + 1) % devices
            ways += [(low, high), (high, low)]
        return ways

    even_ways = pairs(range(0, devices, 2))
    odd_ways = {
        2: pairs(range(1, devices, 4)),
        4: pairs(range(3, devices, 4)),
        6: pairs(range(1, devices, 2)),
    }

    tile = None
    base = 0
    for column_part in column_parts:
        part, tile = column_part(tile)
        even = lax.ppermute(part, "rows", even_ways)
        tile = turn_even(plan, part, even, whole_factors, base, slots, tile)
        base += part.shape[0] // NB

    def exchange(kinds, tile, odd):
        even = unset(tile.shape, tile.dtype)
        far = unset(odd.shape, odd.dtype)
        if kinds & 1:
            even = lax.ppermute(tile, "rows", even_ways)
        if kinds & 6:
            far = lax.ppermute(odd, "rows", odd_ways[kinds & 6])
        return even, far

    branches = [functools.partial(exchange, kinds) for kinds in range(8)]

    def step(t, tile):
        odd = lax.dynamic_slice_in_dim(tile, plan[slots + 1, t] * NB, NB, 0)
        even, odd = lax.switch(plan[slots + 2, t], branches, tile, odd)
        return turn_rows(plan, t, tile, even, odd, whole_factors)

    return lax.fori_loop(1, plan[slots + 3, 0], step, tile)


def gather(factors, windows):
    if lax.axis_size("cols") == 2:
        other = lax.ppermute(factors, "cols", [(0, 1), (1, 0)])
        first = lax.axis_index("cols") == 0
        whole = jnp.concatenate(
            [jnp.where(first, factors, other), jnp.where(first, other, factors)], axis=3
        )
    else:
        whole = lax.all_gather(factors, "cols", axis=3, tiled=True)
    whole = lax.all_gather(whole, "rows", axis=2, tiled=True)
    return whole.reshape((windows,) + whole.shape[2:])


def local(matrix, starts, factors):
    advances, chains = starts.shape
    windows = advances * chains
    blocks = (starts // NB).reshape(windows)
    slots = matrix.shape[0] // NB
    parts = 2 if slots % 2 == 0 else 1
    plan = make_plan(blocks, lax.axis_index("rows"), lax.axis_size("rows"), slots)
    if lax.axis_size("cols") == 2:
        whole = gather(factors, windows)
        packed, came, tables = exchange_columns(matrix, blocks, parts)
        whole, plan, *_ = lax.optimization_barrier((whole, plan, *packed[1:]))

        def column_part(part, tile):
            ghost = came[part]
            if tile is not None:
                ghost, tile = lax.optimization_barrier((ghost, tile))
            return turn_columns(matrix, ghost, whole, *tables, part), tile

        column_parts = [functools.partial(column_part, part) for part in range(parts)]
    else:
        whole = gather(factors, windows)
        tile = columns_of_many(matrix, blocks, whole, chains)
        column_parts = [
            functools.partial(lambda piece, tile: (piece, tile), piece)
            for piece in jnp.split(tile, parts)
        ]
    return turn_all_rows(plan, column_parts, slots, whole)


def solution(mesh):
    return jax.shard_map(
        local,
        mesh=mesh,
        in_specs=(P("rows", "cols"), P(), P(None, None, "rows", "cols")),
        out_specs=P("rows", "cols"),
        check_vma=False,
    )
```

profile of v0, /device:TPU:31, one launch (start us, length us, event | category | flops | bytes accessed | tf_op | source)
XLA Modules:
  0.0 326.3 jit_solution(11471256888564268832)
XLA Ops:
  6.8 4.3 %collective-permute-done.10 = f32[4,4,16,128]{3,2,1,0:T(8,128)S(1)} collective-permute-done((f32[4,4,16,128]{3,2,1,0:T(8,128)}, f32[4,4,16,128]{3,2,1,0:T(8,128)S(1)}, u32[]{:S(2)}, u32[]{:S(2)}) %collective-permute-start.10) | collective-permute-done | bytes 131104 | tf_op jit(solution)/shard_map/ppermute | solution.py:436
  14.2 10.1 %pack_columns.3 = f32[16,256,128]{2,1,0:T(8,128)} custom-call(s32[16]{0:T(128)} %and_select_fusion.slots, f32[512,4096]{1,0:T(8,128)} %tile_ref.7), custom_call_target="tpu_custom_call" | custom-call | bytes 4194304 | tf_op jit(solution)/shard_map/pack_columns/pallas_call | solution.py:36
  24.6 10.2 %pack_columns.2 = f32[16,256,128]{2,1,0:T(8,128)} custom-call(s32[16]{0:T(128)} %and_select_fusion.slots, f32[512,4096]{1,0:T(8,128)} %tile_ref.7), custom_call_target="tpu_custom_call" | custom-call | bytes 4194304 | tf_op jit(solution)/shard_map/pack_columns/pallas_call | solution.py:36
  34.7 2.4 plan_steps.1.plan
  37.9 25.2 %all-gather.2.cloned.1.call-done = f32[4,4,256,256]{3,2,1,0:T(8,128)} async-done(((f32[4,4,16,256]{3,2,1,0:T(8,128)}), f32[4,4,256,256]{3,2,1,0:T(8,128)}) %all-gather.2.cloned.1.call-update) | async-done | bytes 4194320 | tf_op jit(solution)/shard_map/all_gather | solution.py:443
  63.1 7.0 %collective-permute-done.12.ghost_ref = f32[16,256,128]{2,1,0:T(8,128)S(1)} collective-permute-done((f32[16,256,128]{2,1,0:T(8,128)}, f32[16,256,128]{2,1,0:T(8,128)S(1)}, u32[]{:S(2)}, u32[]{:S(2)}) %collective-permute-start.12) | collective-permute-done | bytes 2097184 | tf_op jit(solution)/shard_map/ppermute | solution.py:115
  71.5 11.7 %turn_columns.2.part = f32[256,4096]{1,0:T(8,128)} custom-call(s32[16]{0:T(128)} %and_select_fusion.slots, s32[16]{0:T(128)} %get-tuple-element.63.ghosts, s32[16]{0:T(128)} %copy-done.2, f32[512,4096]{1,0:T(8,128)} %tile_ref.7, f32[16,256,128]{2,1,0:T(8,128)} %copy-done.1, f32[16,256,256]{2,1,0:T(8,128)} %bitcast.12), custom_call_target="tpu_custom_call" | custom-call | flops 1610612736 | bytes 14680064 | tf_op jit(solution)/shard_map/turn_columns/pallas_call | solution.py:80
  83.3 2.4 collective-permute-start.13
  85.9 6.9 %collective-permute-done.13.even = f32[256,4096]{1,0:T(8,128)} collective-permute-done((f32[256,4096]{1,0:T(8,128)}, f32[256,4096]{1,0:T(8,128)}, u32[]{:S(2)}, u32[]{:S(2)}) %collective-permute-start.13) | collective-permute-done | bytes 4194336 | tf_op jit(solution)/shard_map/ppermute | solution.py:411
  92.8 4.3 %turn_even.2.rest_0_ = f32[512,4096]{1,0:T(8,128)} custom-call(s32[8,16]{1,0:T(8,128)S(1)} %plan_steps.1.plan, f32[256,4096]{1,0:T(8,128)} %turn_columns.2.part, f32[256,4096]{1,0:T(8,128)} %collective-permute-done.13.even, f32[16,256,256]{2,1,0:T(8,128)} %bitcast.13), custom_call_target="tpu_custom_call" | custom-call | flops 1610612736 | bytes 12582912 | tf_op jit(solution)/shard_map/turn_even/pallas_call | solution.py:361
  97.1 35.9 %collective-permute-done.11.ghost_ref = f32[16,256,128]{2,1,0:T(8,128)} collective-permute-done((f32[16,256,128]{2,1,0:T(8,128)S(1)}, f32[16,256,128]{2,1,0:T(8,128)}, u32[]{:S(2)}, u32[]{:S(2)}) %collective-permute-start.11) | collective-permute-done | bytes 2097184 | tf_op jit(solution)/shard_map/ppermute | solution.py:115
  132.9 11.6 %turn_columns.3.part = f32[256,4096]{1,0:T(8,128)} custom-call(s32[16]{0:T(128)} %and_select_fusion.slots, s32[16]{0:T(128)} %get-tuple-element.63.ghosts, s32[16]{0:T(128)} %copy-done.2, f32[512,4096]{1,0:T(8,128)} %tile_ref.7, f32[16,256,128]{2,1,0:T(8,128)} %collective-permute-done.11.ghost_ref, f32[16,256,256]{2,1,0:T(8,128)} %bitcast.14), custom_call_target="tpu_custom_call" | custom-call | flops 1610612736 | bytes 14680064 | tf_op jit(solution)/shard_map/turn_columns/pallas_call | solution.py:80
  146.0 6.6 %collective-permute-done.14.even = f32[256,4096]{1,0:T(8,128)} collective-permute-done((f32[256,4096]{1,0:T(8,128)}, f32[256,4096]{1,0:T(8,128)}, u32[]{:S(2)}, u32[]{:S(2)}) %collective-permute-start.14) | collective-permute-done | bytes 4194336 | tf_op jit(solution)/shard_map/ppermute | solution.py:411
  152.5 4.3 %turn_even.3 = f32[512,4096]{1,0:T(8,128)} custom-call(s32[8,16]{1,0:T(8,128)S(1)} %plan_steps.1.plan, f32[256,4096]{1,0:T(8,128)} %turn_columns.3.part, f32[256,4096]{1,0:T(8,128)} %collective-permute-done.14.even, f32[16,256,256]{2,1,0:T(8,128)} %bitcast.15, f32[512,4096]{1,0:T(8,128)} %turn_even.2.rest_0_), custom_call_target="tpu_custom_call", output_to_operand_aliasing={{}: (4, {})} | custom-call | flops 1610612736 | bytes 12582912 | tf_op jit(solution)/shard_map/turn_even/pallas_call | solution.py:361
  156.8 162.6 %while.13 = (s32[]{:T(128)}, f32[512,4096]{1,0:T(8,128)}, s32[]{:T(128)}, s32[8,16]{1,0:T(8,128)S(1)}, f32[16,256,256]{2,1,0:T(8,128)}, /*index=5*/s32[]{:T(128)...) while((s32[]{:T(128)}, f32[512,4096]{1,0:T(8,128)}, ...), condition=%wide.region_10.11_spmd, body=%wide.region_1.10_spmd.sunk | while | flops 10 | bytes 46137692 | solution.py:431
  158.8 1.7 constant_dynamic-slice_fusion.6
  161.3 28.5 %conditional.2 = (f32[512,4096]{1,0:T(8,128)}, f32[128,4096]{1,0:T(8,128)}) conditional(s32[]{:T(128)} %bitcast.10, () %tuple.63, f32[512,4096]{1,0:T(8,128)} %get-tuple-element.153.tile, f32[128,4096]{1,0:T(8,128)S(1)} %constant_dynamic-slice_fusion.6, (f32[512,4096]{1,0:T(8,128)}, ...), branch_computations={%region_2.2_spmd, %region_3.3_spmd, %region_4.4_spmd, %region_5.5_... | conditional | bytes 41943136 | solution.py:428
  161.3 4.2 %collective-permute-start.7 = (f32[128,4096]{1,0:T(8,128)S(1)}, f32[128,4096]{1,0:T(8,128)}, u32[]{:S(2)}, u32[]{:S(2)}) collective-permute-start(f32[128,4096]{1,0:T(8,128)S(1)} %param.6), channel_id=1, source_target_pairs={{2,4},{4,2},{6,8},{8,6},{10,12},{12,10},{14,16},{16,14},{18,20},{2... | collective-permute-start | bytes 6291464 | tf_op jit(solution)/shard_map/while/body/cond/branch_6_fun/ppermute | solution.py:421
  165.5 24.2 %collective-permute-done.7 = f32[128,4096]{1,0:T(8,128)} collective-permute-done((f32[128,4096]{1,0:T(8,128)S(1)}, f32[128,4096]{1,0:T(8,128)}, u32[]{:S(2)}, u32[]{:S(2)}) %collective-permute-start.7) | collective-permute-done | bytes 2097184 | tf_op jit(solution)/shard_map/while/body/cond/branch_6_fun/ppermute | solution.py:421
  189.7 6.1 %turn_rows.1 = f32[512,4096]{1,0:T(8,128)} custom-call(s32[8,16]{1,0:T(8,128)S(1)} %get-tuple-element.167.plan, s32[1]{0:T(128)} %bitcast.9.t_ref, f32[512,4096]{1,0:T(8,128)} %get-tuple-element.153.tile, f32[512,4096]{1,0:T(8,128)} %get-tuple-element.122.even, f32[128,4096]{1,0:T(8,128)} %get-tuple-element.123.odd, ...), custom_call_target="tpu_custom_call", output_to_operand_aliasing={{}: (2, {})} | custom-call | tf_op jit(solution)/shard_map/while/body/turn_rows/pallas_call | solution.py:291
  197.9 1.7 constant_dynamic-slice_fusion.6
  200.3 50.1 %conditional.2 = (f32[512,4096]{1,0:T(8,128)}, f32[128,4096]{1,0:T(8,128)}) conditional(s32[]{:T(128)} %bitcast.10, () %tuple.63, f32[512,4096]{1,0:T(8,128)} %get-tuple-element.153.tile, f32[128,4096]{1,0:T(8,128)S(1)} %constant_dynamic-slice_fusion.6, (f32[512,4096]{1,0:T(8,128)}, ...), branch_computations={%region_2.2_spmd, %region_3.3_spmd, %region_4.4_spmd, %region_5.5_... | conditional | bytes 41943136 | solution.py:428
  200.3 21.7 %collective-permute-start.8 = (f32[512,4096]{1,0:T(8,128)}, f32[512,4096]{1,0:T(8,128)}, u32[]{:S(2)}, u32[]{:S(2)}) collective-permute-start(f32[512,4096]{1,0:T(8,128)} %get-tuple-element.45), channel_id=1, source_target_pairs={{0,2},{2,0},{4,6},{6,4},{8,10},{10,8},{12,14},{14,12},{16,18},{18,... | collective-permute-start | bytes 25165832 | tf_op jit(solution)/shard_map/while/body/cond/branch_7_fun/ppermute | solution.py:419
  222.0 2.4 collective-permute-start.9
  224.4 26.0 %collective-permute-done.9 = f32[128,4096]{1,0:T(8,128)} collective-permute-done((f32[128,4096]{1,0:T(8,128)S(1)}, f32[128,4096]{1,0:T(8,128)}, u32[]{:S(2)}, u32[]{:S(2)}) %collective-permute-start.9) | collective-permute-done | bytes 2097184 | tf_op jit(solution)/shard_map/while/body/cond/branch_7_fun/ppermute | solution.py:421
  250.4 6.1 %turn_rows.1 = f32[512,4096]{1,0:T(8,128)} custom-call(s32[8,16]{1,0:T(8,128)S(1)} %get-tuple-element.167.plan, s32[1]{0:T(128)} %bitcast.9.t_ref, f32[512,4096]{1,0:T(8,128)} %get-tuple-element.153.tile, f32[512,4096]{1,0:T(8,128)} %get-tuple-element.122.even, f32[128,4096]{1,0:T(8,128)} %get-tuple-element.123.odd, ...), custom_call_target="tpu_custom_call", output_to_operand_aliasing={{}: (2, {})} | custom-call | tf_op jit(solution)/shard_map/while/body/turn_rows/pallas_call | solution.py:291
  258.5 1.7 constant_dynamic-slice_fusion.6
  260.9 50.0 %conditional.2 = (f32[512,4096]{1,0:T(8,128)}, f32[128,4096]{1,0:T(8,128)}) conditional(s32[]{:T(128)} %bitcast.10, () %tuple.63, f32[512,4096]{1,0:T(8,128)} %get-tuple-element.153.tile, f32[128,4096]{1,0:T(8,128)S(1)} %constant_dynamic-slice_fusion.6, (f32[512,4096]{1,0:T(8,128)}, ...), branch_computations={%region_2.2_spmd, %region_3.3_spmd, %region_4.4_spmd, %region_5.5_... | conditional | bytes 41943136 | solution.py:428
  261.0 19.8 %collective-permute-start.5 = (f32[512,4096]{1,0:T(8,128)}, f32[512,4096]{1,0:T(8,128)}, u32[]{:S(2)}, u32[]{:S(2)}) collective-permute-start(f32[512,4096]{1,0:T(8,128)} %get-tuple-element.43), channel_id=1, source_target_pairs={{0,2},{2,0},{4,6},{6,4},{8,10},{10,8},{12,14},{14,12},{16,18},{18,... | collective-permute-start | bytes 25165832 | tf_op jit(solution)/shard_map/while/body/cond/branch_5_fun/ppermute | solution.py:419
  280.8 1.9 collective-permute-start.6
  282.7 28.2 %collective-permute-done.6 = f32[128,4096]{1,0:T(8,128)} collective-permute-done((f32[128,4096]{1,0:T(8,128)S(1)}, f32[128,4096]{1,0:T(8,128)}, u32[]{:S(2)}, u32[]{:S(2)}) %collective-permute-start.6) | collective-permute-done | bytes 2097184 | tf_op jit(solution)/shard_map/while/body/cond/branch_5_fun/ppermute | solution.py:421
  310.9 7.8 %turn_rows.1 = f32[512,4096]{1,0:T(8,128)} custom-call(s32[8,16]{1,0:T(8,128)S(1)} %get-tuple-element.167.plan, s32[1]{0:T(128)} %bitcast.9.t_ref, f32[512,4096]{1,0:T(8,128)} %get-tuple-element.153.tile, f32[512,4096]{1,0:T(8,128)} %get-tuple-element.122.even, f32[128,4096]{1,0:T(8,128)} %get-tuple-element.123.odd, ...), custom_call_target="tpu_custom_call", output_to_operand_aliasing={{}: (2, {})} | custom-call | tf_op jit(solution)/shard_map/while/body/turn_rows/pallas_call | solution.py:291
  (28 shorter events, 9.4 us)
Async XLA Ops:
  6.5 56.6 %all-gather.2.cloned.1.call-start = ((), (), s32[]{:S(2)}) async-start(), calls=%async_computation | async-start | bytes 4456448 | tf_op jit(solution)/shard_map/all_gather | solution.py:443
  6.5 4.6 %collective-permute-start.10 = (f32[4,4,16,128]{3,2,1,0:T(8,128)}, f32[4,4,16,128]{3,2,1,0:T(8,128)S(1)}, u32[]{:S(2)}, u32[]{:S(2)}) collective-permute-start(f32[4,4,16,128]{3,2,1,0:T(8,128)} %param.15), channel_id=1, source_target_pairs={{0,1},{1,0},{2,3},{3,2},{4,5},{5,4},{6,7},{7,6},{8,9},{9,8},{10,11... | collective-permute-start | bytes 393224 | tf_op jit(solution)/shard_map/ppermute | solution.py:436
  13.6 10.7 %copy-start.3 = (s32[16]{0:T(128)}, s32[16]{0:T(128)S(1)}, u32[]{:S(2)}) copy-start(s32[16]{0:T(128)S(1)} %reshape.72.blocks) | copy-start | bytes 196
  13.6 10.7 %copy-start.2 = (s32[16]{0:T(128)}, s32[16]{0:T(128)S(1)}, u32[]{:S(2)}) copy-start(s32[16]{0:T(128)S(1)} %get-tuple-element.79.heads) | copy-start | bytes 196
  24.3 45.9 %collective-permute-start.12 = (f32[16,256,128]{2,1,0:T(8,128)}, f32[16,256,128]{2,1,0:T(8,128)S(1)}, u32[]{:S(2)}, u32[]{:S(2)}) collective-permute-start(f32[16,256,128]{2,1,0:T(8,128)} %pack_columns.3), channel_id=1, source_target_pairs={{0,1},{1,0},{2,3},{3,2},{4,5},{5,4},{6,7},{7,6},{8,9},{9,8},{10,11... | collective-permute-start | bytes 6291464 | tf_op jit(solution)/shard_map/ppermute | solution.py:115
  70.2 1.4 copy-start.1
  71.5 14.1 %copy-start = (f32[16,256,128]{2,1,0:T(8,128)S(1)}, f32[16,256,128]{2,1,0:T(8,128)}, u32[]{:S(2)}) copy-start(f32[16,256,128]{2,1,0:T(8,128)} %pack_columns.2) | copy-start | bytes 6291460
  83.3 9.5 %collective-permute-start.13 = (f32[256,4096]{1,0:T(8,128)}, f32[256,4096]{1,0:T(8,128)}, u32[]{:S(2)}, u32[]{:S(2)}) collective-permute-start(f32[256,4096]{1,0:T(8,128)} %turn_columns.2.part), channel_id=1, source_target_pairs={{0,2},{2,0},{4,6},{6,4},{8,10},{10,8},{12,14},{14,12},{16,18},{18,... | collective-permute-start | bytes 12582920 | tf_op jit(solution)/shard_map/ppermute | solution.py:411
  85.7 47.3 %collective-permute-start.11 = (f32[16,256,128]{2,1,0:T(8,128)S(1)}, f32[16,256,128]{2,1,0:T(8,128)}, u32[]{:S(2)}, u32[]{:S(2)}) collective-permute-start(f32[16,256,128]{2,1,0:T(8,128)S(1)} %copy-done), channel_id=1, source_target_pairs={{0,1},{1,0},{2,3},{3,2},{4,5},{5,4},{6,7},{7,6},{8,9},{9,8},{10,11... | collective-permute-start | bytes 6291464 | tf_op jit(solution)/shard_map/ppermute | solution.py:115
  144.5 8.0 %collective-permute-start.14 = (f32[256,4096]{1,0:T(8,128)}, f32[256,4096]{1,0:T(8,128)}, u32[]{:S(2)}, u32[]{:S(2)}) collective-permute-start(f32[256,4096]{1,0:T(8,128)} %turn_columns.3.part), channel_id=1, source_target_pairs={{0,2},{2,0},{4,6},{6,4},{8,10},{10,8},{12,14},{14,12},{16,18},{18,... | collective-permute-start | bytes 12582920 | tf_op jit(solution)/shard_map/ppermute | solution.py:411
  161.3 28.4 %collective-permute-start.7 = (f32[128,4096]{1,0:T(8,128)S(1)}, f32[128,4096]{1,0:T(8,128)}, u32[]{:S(2)}, u32[]{:S(2)}) collective-permute-start(f32[128,4096]{1,0:T(8,128)S(1)} %param.6), channel_id=1, source_target_pairs={{2,4},{4,2},{6,8},{8,6},{10,12},{12,10},{14,16},{16,14},{18,20},{2... | collective-permute-start | bytes 6291464 | tf_op jit(solution)/shard_map/while/body/cond/branch_6_fun/ppermute | solution.py:421
  200.3 50.0 %collective-permute-start.8 = (f32[512,4096]{1,0:T(8,128)}, f32[512,4096]{1,0:T(8,128)}, u32[]{:S(2)}, u32[]{:S(2)}) collective-permute-start(f32[512,4096]{1,0:T(8,128)} %get-tuple-element.45), channel_id=1, source_target_pairs={{0,2},{2,0},{4,6},{6,4},{8,10},{10,8},{12,14},{14,12},{16,18},{18,... | collective-permute-start | bytes 25165832 | tf_op jit(solution)/shard_map/while/body/cond/branch_7_fun/ppermute | solution.py:419
  222.0 28.4 %collective-permute-start.9 = (f32[128,4096]{1,0:T(8,128)S(1)}, f32[128,4096]{1,0:T(8,128)}, u32[]{:S(2)}, u32[]{:S(2)}) collective-permute-start(f32[128,4096]{1,0:T(8,128)S(1)} %get-tuple-element.46), channel_id=1, source_target_pairs={{2,4},{4,2},{6,8},{8,6},{10,12},{12,10},{14,16},{16,14},{18,20},{2... | collective-permute-start | bytes 6291464 | tf_op jit(solution)/shard_map/while/body/cond/branch_7_fun/ppermute | solution.py:421
  261.0 50.0 %collective-permute-start.5 = (f32[512,4096]{1,0:T(8,128)}, f32[512,4096]{1,0:T(8,128)}, u32[]{:S(2)}, u32[]{:S(2)}) collective-permute-start(f32[512,4096]{1,0:T(8,128)} %get-tuple-element.43), channel_id=1, source_target_pairs={{0,2},{2,0},{4,6},{6,4},{8,10},{10,8},{12,14},{14,12},{16,18},{18,... | collective-permute-start | bytes 25165832 | tf_op jit(solution)/shard_map/while/body/cond/branch_5_fun/ppermute | solution.py:419
  280.8 30.1 %collective-permute-start.6 = (f32[128,4096]{1,0:T(8,128)S(1)}, f32[128,4096]{1,0:T(8,128)}, u32[]{:S(2)}, u32[]{:S(2)}) collective-permute-start(f32[128,4096]{1,0:T(8,128)S(1)} %get-tuple-element.44), channel_id=1, source_target_pairs={{6,8},{8,6},{14,16},{16,14},{22,24},{24,22},{30,0},{0,30},{7,9},{9... | collective-permute-start | bytes 6291464 | tf_op jit(solution)/shard_map/while/body/cond/branch_5_fun/ppermute | solution.py:421
Sparse Core Ops, SparseCore 0:
  12.9 50.1 all-gather.1
where the time goes:
time: 327 us; the launch traced here: 326 us
  waiting for transfers between devices  164 us (50%)
  Pallas kernels  74.6 us (23%)
  starting transfers between devices  54 us (17%)
  between operations  13.5 us (4%)
  local copies, waits for them, and re-layouts  9.24 us (3%)
  loops' own time  6.94 us (2%)
  other arithmetic  3.71 us (1%)
    ppermute x3, waiting for transfers between devices, exchange(): far = lax.ppermute(odd, 'rows', odd_ways[kinds & 6])  78.4 us
    ppermute x2, waiting for transfers between devices, exchange_columns(): came.append(lax.ppermute(packed[part], 'cols', [(0, 1), (1, 0)]))  42.9 us
    ppermute x2, starting transfers between devices, exchange(): even = lax.ppermute(tile, 'rows', even_ways)  41.5 us
    all_gather x1, waiting for transfers between devices, gather(): whole = lax.all_gather(whole, 'rows', axis=2, tiled=True)  25.2 us
    pallas_call x2, Pallas kernels, turn_columns(): pl.pallas_call(column_kernel, out_shape=jax.ShapeDtypeStruct((rows, width...  23.3 us
    pallas_call x2, Pallas kernels, pack_columns(): pl.pallas_call(pack_kernel, out_shape=jax.ShapeDtypeStruct((count, rows,...  20.3 us
    pallas_call x3, Pallas kernels, turn_rows(): pl.pallas_call(functools.partial(row_kernel, slots, pieces), out_shape=ja...  20 us
    ppermute x2, waiting for transfers between devices, turn_all_rows(): even = lax.ppermute(part, 'rows', even_ways)  13.4 us
  transfers between devices with their start and end apart: 11, of which 9 were waited for; matrix products, arithmetic and copies ran while one was open for 1% of the time, Pallas kernels for 8%

commit v1 on v0

--- a/solution.py
+++ b/solution.py
@@ -26,22 +26,41 @@
     return dot(lh, rh) + (dot(lh, rl) + dot(ll, rh))
 
 
-def pack_kernel(slots, tile_ref, out_ref):
-    out_ref[0] = tile_ref[...]
+def pack_kernel(part, slots, tile, out, held, load_sem, store_sem):
+    count, rows, _ = held.shape
+
+    def load(w):
+        at = pl.ds(pl.multiple_of(slots[w] * NB, NB), NB)
+        return pltpu.make_async_copy(
+            tile.at[pl.ds(part * rows, rows), at], held.at[w], load_sem.at[w]
+        )
+
+    def store(w):
+        return pltpu.make_async_copy(held.at[w], out.at[w], store_sem.at[w])
+
+    for w in range(count):
+        load(w).start()
+    for w in range(count):
+        load(w).wait()
+        store(w).start()
+    for w in range(count):
+        store(w).wait()
 
 
 def pack_columns(tile, slots, part, parts):
     rows = tile.shape[0] // parts
     count = slots.shape[0]
+    any_space = pl.BlockSpec(memory_space=pl.ANY)
     return pl.pallas_call(
-        pack_kernel,
+        functools.partial(pack_kernel, part),
         out_shape=jax.ShapeDtypeStruct((count, rows, NB), tile.dtype),
-        grid_spec=pltpu.PrefetchScalarGridSpec(
-            num_scalar_prefetch=1,
-            grid=(count,),
-            in_specs=[pl.BlockSpec((rows, NB), lambda w, slots: (part, slots[w]))],
-            out_specs=pl.BlockSpec((1, rows, NB), lambda w, slots: (w, 0, 0)),
-        ),
+        in_specs=[pl.BlockSpec(memory_space=pltpu.SMEM), any_space],
+        out_specs=any_space,
+        scratch_shapes=[
+            pltpu.VMEM((count, rows, NB), tile.dtype),
+            pltpu.SemaphoreType.DMA((count,)),
+            pltpu.SemaphoreType.DMA((count,)),
+        ],
         cost_estimate=pl.CostEstimate(
             flops=0, transcendentals=0, bytes_accessed=8 * count * rows * NB
         ),

time: 327 us -> 320 us (0.979)
  Pallas kernels: 74.6 us -> 60.8 us
  waiting for transfers between devices: 164 us -> 171 us
    pallas_call x2, Pallas kernels: 20.3 us -> 6.55 us  [pack_columns(): pl.pallas_call(functools.partial(pack_kernel, part), out_shape=jax.ShapeD...]
    all_gather x1, waiting for transfers between devices: 25.2 us -> 38.8 us  [gather(): whole = lax.all_gather(whole, 'rows', axis=2, tiled=True)]
    ppermute x2, waiting for transfers between devices: 42.9 us -> 36.2 us  [exchange_columns(): came.append(lax.ppermute(packed[part], 'cols', [(0, 1), (1, 0)]))]
  transfers between devices with their start and end apart: 11 -> 11, of which waited for: 9 -> 9; matrix products, arithmetic and copies ran while one was open for 1% -> 1% of each run, Pallas kernels for 8% -> 4%
where the time goes in v1:
time: 320 us
  waiting for transfers between devices  171 us (53%)
  Pallas kernels  60.8 us (19%)
  starting transfers between devices  54.6 us (17%)
  between operations  13.5 us (4%)
  local copies, waits for them, and re-layouts  9.24 us (3%)
  loops' own time  6.94 us (2%)
  other arithmetic  3.71 us (1%)
    ppermute x3, waiting for transfers between devices, exchange(): far = lax.ppermute(odd, 'rows', odd_ways[kinds & 6])  77.8 us
    ppermute x2, starting transfers between devices, exchange(): even = lax.ppermute(tile, 'rows', even_ways)  41.5 us
    all_gather x1, waiting for transfers between devices, gather(): whole = lax.all_gather(whole, 'rows', axis=2, tiled=True)  38.8 us
    ppermute x2, waiting for transfers between devices, exchange_columns(): came.append(lax.ppermute(packed[part], 'cols', [(0, 1), (1, 0)]))  36.2 us
    pallas_call x2, Pallas kernels, turn_columns(): pl.pallas_call(column_kernel, out_shape=jax.ShapeDtypeStruct((rows, width...  23.3 us
    pallas_call x3, Pallas kernels, turn_rows(): pl.pallas_call(functools.partial(row_kernel, slots, pieces), out_shape=ja...  20 us
    ppermute x2, waiting for transfers between devices, turn_all_rows(): even = lax.ppermute(part, 'rows', even_ways)  13.4 us
    ppermute x3, starting transfers between devices, exchange(): far = lax.ppermute(odd, 'rows', odd_ways[kinds & 6])  9.11 us
  transfers between devices with their start and end apart: 11, of which 9 were waited for; matrix products, arithmetic and copies ran while one was open for 1% of the time, Pallas kernels for 4%

profile of v1, /device:TPU:31, one launch (start us, length us, event | category | flops | bytes accessed | tf_op | source)
XLA Modules:
  0.0 319.5 jit_solution(822802146434204426)
XLA Ops:
  6.8 4.3 %collective-permute-done.10 = f32[4,4,16,128]{3,2,1,0:T(8,128)S(1)} collective-permute-done((f32[4,4,16,128]{3,2,1,0:T(8,128)}, f32[4,4,16,128]{3,2,1,0:T(8,128)S(1)}, u32[]{:S(2)}, u32[]{:S(2)}) %collective-permute-start.10) | collective-permute-done | bytes 131104 | tf_op jit(solution)/shard_map/ppermute | solution.py:455
  14.2 3.3 %pack_columns.3 = f32[16,256,128]{2,1,0:T(8,128)} custom-call(s32[16]{0:T(128)} %and_select_fusion.slots, f32[512,4096]{1,0:T(8,128)} %tile_ref.3), custom_call_target="tpu_custom_call" | custom-call | bytes 4194304 | tf_op jit(solution)/shard_map/pack_columns/pallas_call | solution.py:54
  17.8 3.2 %pack_columns.2 = f32[16,256,128]{2,1,0:T(8,128)} custom-call(s32[16]{0:T(128)} %and_select_fusion.slots, f32[512,4096]{1,0:T(8,128)} %tile_ref.3), custom_call_target="tpu_custom_call" | custom-call | bytes 4194304 | tf_op jit(solution)/shard_map/pack_columns/pallas_call | solution.py:54
  21.1 2.4 plan_steps.1.plan
  24.3 38.8 %all-gather.2.cloned.1.call-done = f32[4,4,256,256]{3,2,1,0:T(8,128)} async-done(((f32[4,4,16,256]{3,2,1,0:T(8,128)}), f32[4,4,256,256]{3,2,1,0:T(8,128)}) %all-gather.2.cloned.1.call-update) | async-done | bytes 4194320 | tf_op jit(solution)/shard_map/all_gather | solution.py:462
  63.5 1.3 copy-done.1
  64.8 11.7 %turn_columns.2.part = f32[256,4096]{1,0:T(8,128)} custom-call(s32[16]{0:T(128)} %and_select_fusion.slots, s32[16]{0:T(128)} %get-tuple-element.63.ghosts, s32[16]{0:T(128)} %copy-done.2, f32[512,4096]{1,0:T(8,128)} %tile_ref.3, f32[16,256,128]{2,1,0:T(8,128)} %copy-done.1, f32[16,256,256]{2,1,0:T(8,128)} %bitcast.12), custom_call_target="tpu_custom_call" | custom-call | flops 1610612736 | bytes 14680064 | tf_op jit(solution)/shard_map/turn_columns/pallas_call | solution.py:99
  76.5 2.4 collective-permute-start.13
  79.2 6.9 %collective-permute-done.13.even = f32[256,4096]{1,0:T(8,128)} collective-permute-done((f32[256,4096]{1,0:T(8,128)}, f32[256,4096]{1,0:T(8,128)}, u32[]{:S(2)}, u32[]{:S(2)}) %collective-permute-start.13) | collective-permute-done | bytes 4194336 | tf_op jit(solution)/shard_map/ppermute | solution.py:430
  86.1 4.3 %turn_even.2.rest_0_ = f32[512,4096]{1,0:T(8,128)} custom-call(s32[8,16]{1,0:T(8,128)S(1)} %plan_steps.1.plan, f32[256,4096]{1,0:T(8,128)} %turn_columns.2.part, f32[256,4096]{1,0:T(8,128)} %collective-permute-done.13.even, f32[16,256,256]{2,1,0:T(8,128)} %bitcast.13), custom_call_target="tpu_custom_call" | custom-call | flops 1610612736 | bytes 12582912 | tf_op jit(solution)/shard_map/turn_even/pallas_call | solution.py:380
  90.3 35.9 %collective-permute-done.11.ghost_ref = f32[16,256,128]{2,1,0:T(8,128)} collective-permute-done((f32[16,256,128]{2,1,0:T(8,128)S(1)}, f32[16,256,128]{2,1,0:T(8,128)}, u32[]{:S(2)}, u32[]{:S(2)}) %collective-permute-start.11) | collective-permute-done | bytes 2097184 | tf_op jit(solution)/shard_map/ppermute | solution.py:134
  126.2 11.6 %turn_columns.3.part = f32[256,4096]{1,0:T(8,128)} custom-call(s32[16]{0:T(128)} %and_select_fusion.slots, s32[16]{0:T(128)} %get-tuple-element.63.ghosts, s32[16]{0:T(128)} %copy-done.2, f32[512,4096]{1,0:T(8,128)} %tile_ref.3, f32[16,256,128]{2,1,0:T(8,128)} %collective-permute-done.11.ghost_ref, f32[16,256,256]{2,1,0:T(8,128)} %bitcast.14), custom_call_target="tpu_custom_call" | custom-call | flops 1610612736 | bytes 14680064 | tf_op jit(solution)/shard_map/turn_columns/pallas_call | solution.py:99
  139.2 6.6 %collective-permute-done.14.even = f32[256,4096]{1,0:T(8,128)} collective-permute-done((f32[256,4096]{1,0:T(8,128)}, f32[256,4096]{1,0:T(8,128)}, u32[]{:S(2)}, u32[]{:S(2)}) %collective-permute-start.14) | collective-permute-done | bytes 4194336 | tf_op jit(solution)/shard_map/ppermute | solution.py:430
  145.8 4.3 %turn_even.3 = f32[512,4096]{1,0:T(8,128)} custom-call(s32[8,16]{1,0:T(8,128)S(1)} %plan_steps.1.plan, f32[256,4096]{1,0:T(8,128)} %turn_columns.3.part, f32[256,4096]{1,0:T(8,128)} %collective-permute-done.14.even, f32[16,256,256]{2,1,0:T(8,128)} %bitcast.15, f32[512,4096]{1,0:T(8,128)} %turn_even.2.rest_0_), custom_call_target="tpu_custom_call", output_to_operand_aliasing={{}: (4, {})} | custom-call | flops 1610612736 | bytes 12582912 | tf_op jit(solution)/shard_map/turn_even/pallas_call | solution.py:380
  150.1 162.6 %while.13 = (s32[]{:T(128)}, f32[512,4096]{1,0:T(8,128)}, s32[]{:T(128)}, s32[8,16]{1,0:T(8,128)S(1)}, f32[16,256,256]{2,1,0:T(8,128)}, /*index=5*/s32[]{:T(128)...) while((s32[]{:T(128)}, f32[512,4096]{1,0:T(8,128)}, ...), condition=%wide.region_10.11_spmd, body=%wide.region_1.10_spmd.sunk | while | flops 10 | bytes 46137692 | solution.py:450
  152.1 1.7 constant_dynamic-slice_fusion.6
  154.5 28.5 %conditional.2 = (f32[512,4096]{1,0:T(8,128)}, f32[128,4096]{1,0:T(8,128)}) conditional(s32[]{:T(128)} %bitcast.10, () %tuple.63, f32[512,4096]{1,0:T(8,128)} %get-tuple-element.153.tile, f32[128,4096]{1,0:T(8,128)S(1)} %constant_dynamic-slice_fusion.6, (f32[512,4096]{1,0:T(8,128)}, ...), branch_computations={%region_2.2_spmd, %region_3.3_spmd, %region_4.4_spmd, %region_5.5_... | conditional | bytes 41943136 | solution.py:447
  154.6 4.5 %collective-permute-start.7 = (f32[128,4096]{1,0:T(8,128)S(1)}, f32[128,4096]{1,0:T(8,128)}, u32[]{:S(2)}, u32[]{:S(2)}) collective-permute-start(f32[128,4096]{1,0:T(8,128)S(1)} %param.6), channel_id=1, source_target_pairs={{2,4},{4,2},{6,8},{8,6},{10,12},{12,10},{14,16},{16,14},{18,20},{2... | collective-permute-start | bytes 6291464 | tf_op jit(solution)/shard_map/while/body/cond/branch_6_fun/ppermute | solution.py:440
  159.1 23.9 %collective-permute-done.7 = f32[128,4096]{1,0:T(8,128)} collective-permute-done((f32[128,4096]{1,0:T(8,128)S(1)}, f32[128,4096]{1,0:T(8,128)}, u32[]{:S(2)}, u32[]{:S(2)}) %collective-permute-start.7) | collective-permute-done | bytes 2097184 | tf_op jit(solution)/shard_map/while/body/cond/branch_6_fun/ppermute | solution.py:440
  183.0 6.1 %turn_rows.1 = f32[512,4096]{1,0:T(8,128)} custom-call(s32[8,16]{1,0:T(8,128)S(1)} %get-tuple-element.167.plan, s32[1]{0:T(128)} %bitcast.9.t_ref, f32[512,4096]{1,0:T(8,128)} %get-tuple-element.153.tile, f32[512,4096]{1,0:T(8,128)} %get-tuple-element.122.even, f32[128,4096]{1,0:T(8,128)} %get-tuple-element.123.odd, ...), custom_call_target="tpu_custom_call", output_to_operand_aliasing={{}: (2, {})} | custom-call | tf_op jit(solution)/shard_map/while/body/turn_rows/pallas_call | solution.py:310
  191.1 1.7 constant_dynamic-slice_fusion.6
  193.6 50.0 %conditional.2 = (f32[512,4096]{1,0:T(8,128)}, f32[128,4096]{1,0:T(8,128)}) conditional(s32[]{:T(128)} %bitcast.10, () %tuple.63, f32[512,4096]{1,0:T(8,128)} %get-tuple-element.153.tile, f32[128,4096]{1,0:T(8,128)S(1)} %constant_dynamic-slice_fusion.6, (f32[512,4096]{1,0:T(8,128)}, ...), branch_computations={%region_2.2_spmd, %region_3.3_spmd, %region_4.4_spmd, %region_5.5_... | conditional | bytes 41943136 | solution.py:447
  193.6 21.6 %collective-permute-start.8 = (f32[512,4096]{1,0:T(8,128)}, f32[512,4096]{1,0:T(8,128)}, u32[]{:S(2)}, u32[]{:S(2)}) collective-permute-start(f32[512,4096]{1,0:T(8,128)} %get-tuple-element.45), channel_id=1, source_target_pairs={{0,2},{2,0},{4,6},{6,4},{8,10},{10,8},{12,14},{14,12},{16,18},{18,... | collective-permute-start | bytes 25165832 | tf_op jit(solution)/shard_map/while/body/cond/branch_7_fun/ppermute | solution.py:438
  215.3 2.7 collective-permute-start.9
  218.0 25.7 %collective-permute-done.9 = f32[128,4096]{1,0:T(8,128)} collective-permute-done((f32[128,4096]{1,0:T(8,128)S(1)}, f32[128,4096]{1,0:T(8,128)}, u32[]{:S(2)}, u32[]{:S(2)}) %collective-permute-start.9) | collective-permute-done | bytes 2097184 | tf_op jit(solution)/shard_map/while/body/cond/branch_7_fun/ppermute | solution.py:440
  243.6 6.1 %turn_rows.1 = f32[512,4096]{1,0:T(8,128)} custom-call(s32[8,16]{1,0:T(8,128)S(1)} %get-tuple-element.167.plan, s32[1]{0:T(128)} %bitcast.9.t_ref, f32[512,4096]{1,0:T(8,128)} %get-tuple-element.153.tile, f32[512,4096]{1,0:T(8,128)} %get-tuple-element.122.even, f32[128,4096]{1,0:T(8,128)} %get-tuple-element.123.odd, ...), custom_call_target="tpu_custom_call", output_to_operand_aliasing={{}: (2, {})} | custom-call | tf_op jit(solution)/shard_map/while/body/turn_rows/pallas_call | solution.py:310
  251.8 1.7 constant_dynamic-slice_fusion.6
  254.2 50.0 %conditional.2 = (f32[512,4096]{1,0:T(8,128)}, f32[128,4096]{1,0:T(8,128)}) conditional(s32[]{:T(128)} %bitcast.10, () %tuple.63, f32[512,4096]{1,0:T(8,128)} %get-tuple-element.153.tile, f32[128,4096]{1,0:T(8,128)S(1)} %constant_dynamic-slice_fusion.6, (f32[512,4096]{1,0:T(8,128)}, ...), branch_computations={%region_2.2_spmd, %region_3.3_spmd, %region_4.4_spmd, %region_5.5_... | conditional | bytes 41943136 | solution.py:447
  254.2 19.8 %collective-permute-start.5 = (f32[512,4096]{1,0:T(8,128)}, f32[512,4096]{1,0:T(8,128)}, u32[]{:S(2)}, u32[]{:S(2)}) collective-permute-start(f32[512,4096]{1,0:T(8,128)} %get-tuple-element.43), channel_id=1, source_target_pairs={{0,2},{2,0},{4,6},{6,4},{8,10},{10,8},{12,14},{14,12},{16,18},{18,... | collective-permute-start | bytes 25165832 | tf_op jit(solution)/shard_map/while/body/cond/branch_5_fun/ppermute | solution.py:438
  274.1 1.9 collective-permute-start.6
  276.0 28.2 %collective-permute-done.6 = f32[128,4096]{1,0:T(8,128)} collective-permute-done((f32[128,4096]{1,0:T(8,128)S(1)}, f32[128,4096]{1,0:T(8,128)}, u32[]{:S(2)}, u32[]{:S(2)}) %collective-permute-start.6) | collective-permute-done | bytes 2097184 | tf_op jit(solution)/shard_map/while/body/cond/branch_5_fun/ppermute | solution.py:440
  304.2 7.8 %turn_rows.1 = f32[512,4096]{1,0:T(8,128)} custom-call(s32[8,16]{1,0:T(8,128)S(1)} %get-tuple-element.167.plan, s32[1]{0:T(128)} %bitcast.9.t_ref, f32[512,4096]{1,0:T(8,128)} %get-tuple-element.153.tile, f32[512,4096]{1,0:T(8,128)} %get-tuple-element.122.even, f32[128,4096]{1,0:T(8,128)} %get-tuple-element.123.odd, ...), custom_call_target="tpu_custom_call", output_to_operand_aliasing={{}: (2, {})} | custom-call | tf_op jit(solution)/shard_map/while/body/turn_rows/pallas_call | solution.py:310
  (28 shorter events, 8.4 us)
Async XLA Ops:
  6.5 56.6 %all-gather.2.cloned.1.call-start = ((), (), s32[]{:S(2)}) async-start(), calls=%async_computation | async-start | bytes 4456448 | tf_op jit(solution)/shard_map/all_gather | solution.py:462
  6.5 4.6 %collective-permute-start.10 = (f32[4,4,16,128]{3,2,1,0:T(8,128)}, f32[4,4,16,128]{3,2,1,0:T(8,128)S(1)}, u32[]{:S(2)}, u32[]{:S(2)}) collective-permute-start(f32[4,4,16,128]{3,2,1,0:T(8,128)} %param.15), channel_id=1, source_target_pairs={{0,1},{1,0},{2,3},{3,2},{4,5},{5,4},{6,7},{7,6},{8,9},{9,8},{10,11... | collective-permute-start | bytes 393224 | tf_op jit(solution)/shard_map/ppermute | solution.py:455
  13.6 3.9 %copy-start.3 = (s32[16]{0:T(128)}, s32[16]{0:T(128)S(1)}, u32[]{:S(2)}) copy-start(s32[16]{0:T(128)S(1)} %reshape.72.blocks) | copy-start | bytes 196
  13.6 3.9 %copy-start.2 = (s32[16]{0:T(128)}, s32[16]{0:T(128)S(1)}, u32[]{:S(2)}) copy-start(s32[16]{0:T(128)S(1)} %get-tuple-element.79.heads) | copy-start | bytes 196
  17.5 45.9 %collective-permute-start.12 = (f32[16,256,128]{2,1,0:T(8,128)}, f32[16,256,128]{2,1,0:T(8,128)S(1)}, u32[]{:S(2)}, u32[]{:S(2)}) collective-permute-start(f32[16,256,128]{2,1,0:T(8,128)} %pack_columns.3), channel_id=1, source_target_pairs={{0,1},{1,0},{2,3},{3,2},{4,5},{5,4},{6,7},{7,6},{8,9},{9,8},{10,11... | collective-permute-start | bytes 6291464 | tf_op jit(solution)/shard_map/ppermute | solution.py:134
  63.5 1.4 copy-start.1
  64.8 14.1 %copy-start = (f32[16,256,128]{2,1,0:T(8,128)S(1)}, f32[16,256,128]{2,1,0:T(8,128)}, u32[]{:S(2)}) copy-start(f32[16,256,128]{2,1,0:T(8,128)} %pack_columns.2) | copy-start | bytes 6291460
  76.5 9.5 %collective-permute-start.13 = (f32[256,4096]{1,0:T(8,128)}, f32[256,4096]{1,0:T(8,128)}, u32[]{:S(2)}, u32[]{:S(2)}) collective-permute-start(f32[256,4096]{1,0:T(8,128)} %turn_columns.2.part), channel_id=1, source_target_pairs={{0,2},{2,0},{4,6},{6,4},{8,10},{10,8},{12,14},{14,12},{16,18},{18,... | collective-permute-start | bytes 12582920 | tf_op jit(solution)/shard_map/ppermute | solution.py:430
  78.9 47.3 %collective-permute-start.11 = (f32[16,256,128]{2,1,0:T(8,128)S(1)}, f32[16,256,128]{2,1,0:T(8,128)}, u32[]{:S(2)}, u32[]{:S(2)}) collective-permute-start(f32[16,256,128]{2,1,0:T(8,128)S(1)} %copy-done), channel_id=1, source_target_pairs={{0,1},{1,0},{2,3},{3,2},{4,5},{5,4},{6,7},{7,6},{8,9},{9,8},{10,11... | collective-permute-start | bytes 6291464 | tf_op jit(solution)/shard_map/ppermute | solution.py:134
  137.8 8.0 %collective-permute-start.14 = (f32[256,4096]{1,0:T(8,128)}, f32[256,4096]{1,0:T(8,128)}, u32[]{:S(2)}, u32[]{:S(2)}) collective-permute-start(f32[256,4096]{1,0:T(8,128)} %turn_columns.3.part), channel_id=1, source_target_pairs={{0,2},{2,0},{4,6},{6,4},{8,10},{10,8},{12,14},{14,12},{16,18},{18,... | collective-permute-start | bytes 12582920 | tf_op jit(solution)/shard_map/ppermute | solution.py:430
  154.6 28.4 %collective-permute-start.7 = (f32[128,4096]{1,0:T(8,128)S(1)}, f32[128,4096]{1,0:T(8,128)}, u32[]{:S(2)}, u32[]{:S(2)}) collective-permute-start(f32[128,4096]{1,0:T(8,128)S(1)} %param.6), channel_id=1, source_target_pairs={{2,4},{4,2},{6,8},{8,6},{10,12},{12,10},{14,16},{16,14},{18,20},{2... | collective-permute-start | bytes 6291464 | tf_op jit(solution)/shard_map/while/body/cond/branch_6_fun/ppermute | solution.py:440
  193.6 50.0 %collective-permute-start.8 = (f32[512,4096]{1,0:T(8,128)}, f32[512,4096]{1,0:T(8,128)}, u32[]{:S(2)}, u32[]{:S(2)}) collective-permute-start(f32[512,4096]{1,0:T(8,128)} %get-tuple-element.45), channel_id=1, source_target_pairs={{0,2},{2,0},{4,6},{6,4},{8,10},{10,8},{12,14},{14,12},{16,18},{18,... | collective-permute-start | bytes 25165832 | tf_op jit(solution)/shard_map/while/body/cond/branch_7_fun/ppermute | solution.py:438
  215.3 28.4 %collective-permute-start.9 = (f32[128,4096]{1,0:T(8,128)S(1)}, f32[128,4096]{1,0:T(8,128)}, u32[]{:S(2)}, u32[]{:S(2)}) collective-permute-start(f32[128,4096]{1,0:T(8,128)S(1)} %get-tuple-element.46), channel_id=1, source_target_pairs={{2,4},{4,2},{6,8},{8,6},{10,12},{12,10},{14,16},{16,14},{18,20},{2... | collective-permute-start | bytes 6291464 | tf_op jit(solution)/shard_map/while/body/cond/branch_7_fun/ppermute | solution.py:440
  254.2 50.0 %collective-permute-start.5 = (f32[512,4096]{1,0:T(8,128)}, f32[512,4096]{1,0:T(8,128)}, u32[]{:S(2)}, u32[]{:S(2)}) collective-permute-start(f32[512,4096]{1,0:T(8,128)} %get-tuple-element.43), channel_id=1, source_target_pairs={{0,2},{2,0},{4,6},{6,4},{8,10},{10,8},{12,14},{14,12},{16,18},{18,... | collective-permute-start | bytes 25165832 | tf_op jit(solution)/shard_map/while/body/cond/branch_5_fun/ppermute | solution.py:438
  274.1 30.1 %collective-permute-start.6 = (f32[128,4096]{1,0:T(8,128)S(1)}, f32[128,4096]{1,0:T(8,128)}, u32[]{:S(2)}, u32[]{:S(2)}) collective-permute-start(f32[128,4096]{1,0:T(8,128)S(1)} %get-tuple-element.44), channel_id=1, source_target_pairs={{6,8},{8,6},{14,16},{16,14},{22,24},{24,22},{30,0},{0,30},{7,9},{9... | collective-permute-start | bytes 6291464 | tf_op jit(solution)/shard_map/while/body/cond/branch_5_fun/ppermute | solution.py:440
Sparse Core Ops, SparseCore 0:
  12.9 50.1 all-gather.1
